TPU v7x, 32 devices: a whole 2x2x4 slice. The times are simulated.
32 devices in a mesh: bl: 4 (over y, x), freq: 8 (over z, core).
Axes of the slice: x: 2, y: 2, z: 4, core: 2. Of those that a mesh axis runs over, the one named last changes fastest.
Arguments:
- visibilities: float32 [2, 2, 128, 8192], P(None, None, 'freq', 'bl'), may hold values from -8 to 8
- sample_flag_weight: int32 [2, 128, 8192], P(None, 'freq', 'bl'), may hold values from 0 to 4
- baseline_station_pair: int32 [2, 8192], P(None, 'bl'), may hold values from 0 to 511, as said below
- baseline_spatial_coords: float32 [2, 2, 8192], P(None, None, 'bl'), may hold values from -6 to 6
- directions: float32 [2, 8], replicated, may hold values from -0.5 to 0.5
- source_flux: float32 [8, 128], P(None, 'freq'), may hold values from 0.5 to 2
- channel_ratio: float32 [128], P('freq'), may hold values from 0.7 to 1.4
- jones_gains: float32 [2, 8, 128, 512], P(None, None, 'freq'), may hold values from -4 to 4
- scaled_dual: float32 [2, 8, 128, 512], P(None, None, 'freq'), may hold values from -2 to 2
- consensus: float32 [2, 3, 8, 512], replicated, may hold values from -3 to 3
- penalty: float32 [8], replicated, may hold values from 0.3 to 3
Outputs:
- new_gains: float32 [2, 8, 128, 512], P(None, None, 'freq')
- new_consensus: float32 [2, 3, 8, 512], replicated
- new_dual: float32 [2, 8, 128, 512], P(None, None, 'freq')
- residuals: float32 [2, 2, 128, 8192], P(None, None, 'freq', 'bl')
Inputs may be any that keep to these rules, and one draw needn't show every extreme that they name: `baseline_station_pair`: the two stations of every baseline differ.
All inputs are finite; a program needn't handle non-finite values.
Results may differ from a plain program's by a relative error of at most 0.00016.
Values sent between devices are 32-bit elements; how exact they have to be, the bound alone decides.
A program may use at most 64 MiB of HBM per device.

v0:
```python
import math

import jax
import jax.numpy as jnp
from jax import lax
from jax.sharding import PartitionSpec as P

NPOLY = 3
ITERS = 3


robust_dof = 2.0
small_term = 1e-06
two_pi = 2.0 * math.pi


def legendre(ratios):
    scaled = (ratios - 1.05) / 0.35
    values = [jnp.ones_like(scaled), scaled]
    values.append((3 * scaled * values[1] - 1 * values[0]) / 2)
    return jnp.stack(values[:NPOLY])


def coherency(coords, sky_dirs, fluxes, ratios):
    project = (
        sky_dirs[0][:, None, None] * coords[0][None] + sky_dirs[1][:, None, None] * coords[1][None]
    )
    phases = two_pi * project[:, :, None, :] * ratios[None, None, :, None]
    amplitude = fluxes[:, None, :, None]
    return (amplitude * jnp.cos(phases), amplitude * jnp.sin(phases))


def station_table(pair_row, station_list):
    positions = lax.broadcasted_iota(jnp.int32, (station_list, pair_row.shape[0]), 0)
    return (positions == pair_row[None, :]).astype(jnp.float32)


def pick_stations(gain_re, gain_im, table):
    stacked = jnp.stack([gain_re, gain_im])
    lead_shape = stacked.shape[:3]
    flat = stacked.reshape(-1, stacked.shape[3])
    picked = jnp.dot(
        flat, table, precision=lax.Precision.HIGHEST, preferred_element_type=jnp.float32
    )
    picked = picked.reshape(lead_shape + (table.shape[1],))
    return (picked[0], picked[1])


def predict(gain_re, gain_im, left_table, right_table, sky_re, sky_im):
    left_re, left_im = pick_stations(gain_re, gain_im, left_table)
    right_re, right_im = pick_stations(gain_re, gain_im, right_table)
    pair_re = left_re * right_re + left_im * right_im
    pair_im = left_im * right_re - left_re * right_im
    model_re = pair_re[:, None] * sky_re - pair_im[:, None] * sky_im
    model_im = pair_re[:, None] * sky_im + pair_im[:, None] * sky_re
    return ((left_re, left_im, right_re, right_im), model_re, model_im)


def residual_of(observed, model_re, model_im):
    return (observed[0] - jnp.sum(model_re, axis=0), observed[1] - jnp.sum(model_im, axis=0))


def robust_weights(flagged, error_re, error_im, sigma_sq):
    return (
        flagged
        * (robust_dof + 1.0)
        / (robust_dof + (error_re * error_re + error_im * error_im) / sigma_sq)
    )


def normal_terms(
    error_re,
    error_im,
    model_re,
    model_im,
    weights,
    sky_re,
    sky_im,
    side_gains,
    left_table,
    right_table,
):
    target_re = error_re[None] + model_re
    target_im = error_im[None] + model_im
    cross_re = sky_re * target_re + sky_im * target_im
    cross_im = sky_re * target_im - sky_im * target_re
    weight_wide = weights[None]
    summed_re = jnp.sum(weight_wide * cross_re, axis=1)
    summed_im = jnp.sum(weight_wide * cross_im, axis=1)
    powers = jnp.sum(weight_wide * (sky_re * sky_re + sky_im * sky_im), axis=1)
    left_re, left_im, right_re, right_im = side_gains
    first_re = right_re * summed_re - right_im * summed_im
    first_im = right_re * summed_im + right_im * summed_re
    second_re = left_re * summed_re + left_im * summed_im
    second_im = left_im * summed_re - left_re * summed_im
    first_norm = (right_re * right_re + right_im * right_im) * powers
    second_norm = (left_re * left_re + left_im * left_im) * powers
    stacked_first = jnp.stack([first_re, first_im, first_norm])
    stacked_second = jnp.stack([second_re, second_im, second_norm])
    lead_shape = stacked_first.shape[:3]
    baseline_count = stacked_first.shape[3]
    contract = (((1,), (1,)), ((), ()))
    into_first = lax.dot_general(
        stacked_first.reshape(-1, baseline_count),
        left_table,
        contract,
        precision=lax.Precision.HIGHEST,
        preferred_element_type=jnp.float32,
    )
    into_second = lax.dot_general(
        stacked_second.reshape(-1, baseline_count),
        right_table,
        contract,
        precision=lax.Precision.HIGHEST,
        preferred_element_type=jnp.float32,
    )
    return (into_first + into_second).reshape(lead_shape + (left_table.shape[0],))


def update_gains(gain_re, gain_im, normal_sums, anchor_re, anchor_im, effective_penalty):
    penalty_wide = effective_penalty[:, None, None]
    divisor = normal_sums[2] + penalty_wide
    solved_re = (normal_sums[0] + penalty_wide * anchor_re) / divisor
    solved_im = (normal_sums[1] + penalty_wide * anchor_im) / divisor
    return (0.5 * (gain_re + solved_re), 0.5 * (gain_im + solved_im))


def cholesky_solve(gram_total, flat_rhs):
    factor = jnp.linalg.cholesky(gram_total)
    matrix_order = gram_total.shape[0]
    forward = []
    for row_index in range(matrix_order):
        running = flat_rhs[row_index]
        for col_index in range(row_index):
            running = running - factor[row_index, col_index] * forward[col_index]
        forward.append(running / factor[row_index, row_index])
    backward = [None] * matrix_order
    for row_index in reversed(range(matrix_order)):
        running = forward[row_index]
        for col_index in range(row_index + 1, matrix_order):
            running = running - factor[col_index, row_index] * backward[col_index]
        backward[row_index] = running / factor[row_index, row_index]
    return jnp.stack(backward)


def solve_consensus(gram_total, rhs_total):
    matrix_order = gram_total.shape[0]
    flat_rhs = jnp.moveaxis(rhs_total, 1, 0).reshape(matrix_order, -1)
    solved = cholesky_solve(gram_total, flat_rhs)
    return jnp.moveaxis(
        solved.reshape((matrix_order, rhs_total.shape[0]) + rhs_total.shape[2:]), 0, 1
    )


def body(
    visibilities,
    sample_flag_weight,
    baseline_station_pair,
    baseline_spatial_coords,
    directions,
    source_flux,
    channel_ratio,
    jones_gains,
    scaled_dual,
    consensus,
    penalty,
):
    station_list = jones_gains.shape[3]
    baseline_list = baseline_station_pair.shape[1] * lax.axis_size("bl")
    solution_time_slots = visibilities.shape[1]
    effective_penalty = penalty * (2.0 * baseline_list * solution_time_slots / station_list)
    left_table = station_table(baseline_station_pair[0], station_list)
    right_table = station_table(baseline_station_pair[1], station_list)
    sky_re, sky_im = coherency(baseline_spatial_coords, directions, source_flux, channel_ratio)
    poly_basis = legendre(channel_ratio)
    gram_local = jnp.dot(poly_basis, poly_basis.T, precision=lax.Precision.HIGHEST)
    anchor = (
        jnp.einsum("jc,xjks->xkcs", poly_basis, consensus, precision=lax.Precision.HIGHEST)
        - scaled_dual
    )
    anchor_re, anchor_im = (anchor[0], anchor[1])
    flagged = sample_flag_weight.astype(jnp.float32)
    count_local = jnp.sum(flagged)
    gain_re, gain_im = (jones_gains[0], jones_gains[1])
    for iteration in range(ITERS):
        side_gains, model_re, model_im = predict(
            gain_re, gain_im, left_table, right_table, sky_re, sky_im
        )
        error_re, error_im = residual_of(visibilities, model_re, model_im)
        misfit_local = jnp.sum(flagged * (error_re * error_re + error_im * error_im))
        squares, weight_total = lax.psum((misfit_local, count_local), ("bl", "freq"))
        sigma_sq = squares / (weight_total + 1.0) + small_term
        weights = robust_weights(flagged, error_re, error_im, sigma_sq)
        partial_value = normal_terms(
            error_re,
            error_im,
            model_re,
            model_im,
            weights,
            sky_re,
            sky_im,
            side_gains,
            left_table,
            right_table,
        )
        owned_sums = lax.psum_scatter(partial_value, "bl", scatter_dimension=3, tiled=True)
        own_width = owned_sums.shape[3]
        offset = lax.axis_index("bl") * own_width
        own_gain_re = lax.dynamic_slice_in_dim(gain_re, offset, own_width, 2)
        own_gain_im = lax.dynamic_slice_in_dim(gain_im, offset, own_width, 2)
        own_anchor_re = lax.dynamic_slice_in_dim(anchor_re, offset, own_width, 2)
        own_anchor_im = lax.dynamic_slice_in_dim(anchor_im, offset, own_width, 2)
        new_re, new_im = update_gains(
            own_gain_re, own_gain_im, owned_sums, own_anchor_re, own_anchor_im, effective_penalty
        )
        gathered = lax.all_gather(jnp.stack([new_re, new_im]), "bl", axis=3, tiled=True)
        gain_re, gain_im = (gathered[0], gathered[1])
    side_gains, model_re, model_im = predict(
        gain_re, gain_im, left_table, right_table, sky_re, sky_im
    )
    error_re, error_im = residual_of(visibilities, model_re, model_im)
    residuals = jnp.stack([error_re, error_im])
    new_gains = jnp.stack([gain_re, gain_im])
    rhs_local = jnp.einsum(
        "jc,xkcs->xjks", poly_basis, new_gains + scaled_dual, precision=lax.Precision.HIGHEST
    )
    rhs_total, gram_total = lax.psum((rhs_local, gram_local), "freq")
    new_consensus = solve_consensus(gram_total, rhs_total)
    new_dual = (
        scaled_dual
        + new_gains
        - jnp.einsum("jc,xjks->xkcs", poly_basis, new_consensus, precision=lax.Precision.HIGHEST)
    )
    return (new_gains, new_consensus, new_dual, residuals)


def solution(mesh):
    in_specs = (
        P(None, None, "freq", "bl"),
        P(None, "freq", "bl"),
        P(None, "bl"),
        P(None, None, "bl"),
        P(),
        P(None, "freq"),
        P("freq"),
        P(None, None, "freq", None),
        P(None, None, "freq", None),
        P(),
        P(),
    )
    out_specs = (
        P(None, None, "freq", None),
        P(),
        P(None, None, "freq", None),
        P(None, None, "freq", "bl"),
    )
    return jax.shard_map(body, mesh=mesh, in_specs=in_specs, out_specs=out_specs, check_vma=False)
```

profile of v0, /device:TPU:0, one launch (start us, length us, event | category | flops | bytes accessed | tf_op | source)
XLA Modules:
  0.0 447.5 jit_solution(5179471884949867166)
XLA Ops:
  8.1 3.2 fusion.14
  13.5 2.4 multiply_add_fusion.3
  16.0 9.0 %fusion.102 = (f32[2,16,2048]{2,1,0:T(8,128)S(1)}, f32[2,16,2048]{2,1,0:T(8,128)S(1)}) fusion(f32[8,16,2048]{2,1,0:T(8,128)S(1)} %bitcast.263, f32[16]{0:T(128)S(1)} %copy-done.28, f32[8,2,2048]{2,1,0:T(2,128)S(1)} %add_multiply_fusion, f32[8,16]{1,0:T(8,128)S(1)} %copy-done.26, f32[8,16,2048]{2,1,0:T(8,128)S(1)} %bitcast.261), kind=kLoop, calls=%fused_computation.115 | loop fusion | flops 5636096 | bytes 2753088 | tf_op jit(solution)/shard_map/reduce_sum | solution.py:60
  27.2 42.8 %all-reduce = (f32[]{:T(128)}, f32[]{:T(128)}) all-reduce(f32[]{:T(128)} %get-tuple-element.34, f32[]{:T(128)} %get-tuple-element.33), channel_id=1, replica_groups=mesh['bl'=4,'freq'=8] {'bl','freq'}, use_global_device_ids=true, to_apply=%region_3.0 | all-reduce | flops 2 | bytes 16 | tf_op jit(solution)/shard_map/psum | solution.py:191
  72.3 10.9 %fusion.36 = (f32[8,16,2048]{2,1,0:T(8,128)S(1)}, f32[8,16,2048]{2,1,0:T(8,128)S(1)}, f32[8,16,2048]{2,1,0:T(8,128)S(1)}) fusion(f32[2,16,2048]{2,1,0:T(8,128)} %get-tuple-element.104, f32[2,16,2048]{2,1,0:T(8,128)S(1)} %get-tuple-element.103, f32[2,16,2048]{2,1,0:T(8,128)S(1)} %add_divide_fusion.2, f32[8,16,2048]{2,1,0:T(8,128)S(1)} %bitcast.264, ...), kind=kLoop, calls=%fused_computation.46 | loop fusion | flops 12845056 | bytes 6160960 | tf_op jit(solution)/shard_map/reduce_sum | solution.py:88
  85.6 3.0 fusion.5
  88.6 3.9 fusion.103
  94.4 24.4 %reduce-scatter.4.cloned.1.call-done = f32[3,8,16,128]{3,2,1,0:T(8,128)} async-done(((f32[3,8,16,512]{3,2,1,0:T(8,128)}), f32[3,8,16,128]{3,2,1,0:T(8,128)}) %reduce-scatter.4.cloned.1.call-update) | async-done | bytes 196624 | tf_op jit(solution)/shard_map/reduce_scatter | solution.py:206
  119.9 13.2 %all_gather.9 = f32[2,8,16,512]{3,2,1,0:T(8,128)S(1)} all-gather(f32[2,8,16,128]{3,2,1,0:T(8,128)S(1)} %pad_maximum_fusion.7), channel_id=1, replica_groups=mesh['bl'=4,'freq'=8] {'bl'}, dimensions={3}, use_global_device_ids=true | all-gather | bytes 655360 | tf_op jit(solution)/shard_map/all_gather | solution.py:216
  137.4 2.4 multiply_add_fusion.2
  139.8 9.0 %fusion.98 = (f32[2,16,2048]{2,1,0:T(8,128)S(1)}, f32[2,16,2048]{2,1,0:T(8,128)S(1)}) fusion(f32[8,16,2048]{2,1,0:T(8,128)S(1)} %bitcast.271, f32[8,16,2048]{2,1,0:T(8,128)S(1)} %bitcast.269, f32[16]{0:T(128)S(1)} %copy-done.28, f32[8,2,2048]{2,1,0:T(2,128)S(1)} %add_multiply_fusion, f32[8,16]{1,0:T(8,128)S(1)} %copy-done.26), kind=kLoop, calls=%fused_computation.111 | loop fusion | flops 5636096 | bytes 2753088 | tf_op jit(solution)/shard_map/reduce_sum | solution.py:60
  150.9 39.7 %psum.50 = f32[]{:T(128)} all-reduce(f32[]{:T(128)} %get-tuple-element.42), channel_id=1, replica_groups=mesh['bl'=4,'freq'=8] {'bl','freq'}, use_global_device_ids=true, to_apply=%region_13.0 | all-reduce | flops 1 | bytes 8 | tf_op jit(solution)/shard_map/psum | solution.py:191
  192.4 10.9 %fusion.45 = (f32[8,16,2048]{2,1,0:T(8,128)S(1)}, f32[8,16,2048]{2,1,0:T(8,128)S(1)}, f32[8,16,2048]{2,1,0:T(8,128)S(1)}) fusion(f32[2,16,2048]{2,1,0:T(8,128)} %get-tuple-element.98, f32[2,16,2048]{2,1,0:T(8,128)S(1)} %get-tuple-element.97, f32[2,16,2048]{2,1,0:T(8,128)S(1)} %add_divide_fusion.1, f32[8,16,2048]{2,1,0:T(8,128)S(1)} %bitcast.272, ...), kind=kLoop, calls=%fused_computation.55 | loop fusion | flops 12845056 | bytes 6160960 | tf_op jit(solution)/shard_map/reduce_sum | solution.py:88
  205.0 3.0 fusion.3
  208.4 3.9 fusion.104
  212.5 26.2 %reduce-scatter.6.cloned.1.call-done = f32[3,8,16,128]{3,2,1,0:T(8,128)} async-done(((f32[3,8,16,512]{3,2,1,0:T(8,128)}), f32[3,8,16,128]{3,2,1,0:T(8,128)}) %reduce-scatter.6.cloned.1.call-update) | async-done | bytes 196624 | tf_op jit(solution)/shard_map/reduce_scatter | solution.py:206
  239.8 13.3 %all_gather.10 = f32[2,8,16,512]{3,2,1,0:T(8,128)S(1)} all-gather(f32[2,8,16,128]{3,2,1,0:T(8,128)S(1)} %pad_maximum_fusion.8), channel_id=1, replica_groups=mesh['bl'=4,'freq'=8] {'bl'}, dimensions={3}, use_global_device_ids=true | all-gather | bytes 655360 | tf_op jit(solution)/shard_map/all_gather | solution.py:216
  257.3 2.4 multiply_add_fusion.1
  259.7 9.0 %fusion.94 = (f32[2,16,2048]{2,1,0:T(8,128)S(1)}, f32[2,16,2048]{2,1,0:T(8,128)S(1)}) fusion(f32[8,16,2048]{2,1,0:T(8,128)S(1)} %bitcast.267, f32[8,16,2048]{2,1,0:T(8,128)S(1)} %bitcast.265, f32[16]{0:T(128)S(1)} %copy-done.28, f32[8,2,2048]{2,1,0:T(2,128)S(1)} %add_multiply_fusion, f32[8,16]{1,0:T(8,128)S(1)} %copy-done.26), kind=kLoop, calls=%fused_computation.107 | loop fusion | flops 5636096 | bytes 2753088 | tf_op jit(solution)/shard_map/reduce_sum | solution.py:60
  270.9 40.0 %psum.51 = f32[]{:T(128)} all-reduce(f32[]{:T(128)} %get-tuple-element.40), channel_id=1, replica_groups=mesh['bl'=4,'freq'=8] {'bl','freq'}, use_global_device_ids=true, to_apply=%region_21.0 | all-reduce | flops 1 | bytes 8 | tf_op jit(solution)/shard_map/psum | solution.py:191
  312.6 10.9 %fusion.53 = (f32[8,16,2048]{2,1,0:T(8,128)S(1)}, f32[8,16,2048]{2,1,0:T(8,128)S(1)}, f32[8,16,2048]{2,1,0:T(8,128)S(1)}) fusion(f32[2,16,2048]{2,1,0:T(8,128)} %get-tuple-element.94, f32[2,16,2048]{2,1,0:T(8,128)S(1)} %get-tuple-element.93, f32[2,16,2048]{2,1,0:T(8,128)S(1)} %add_divide_fusion, f32[8,16,2048]{2,1,0:T(8,128)S(1)} %bitcast.268, ...), kind=kLoop, calls=%fused_computation.63 | loop fusion | flops 12845056 | bytes 6160960 | tf_op jit(solution)/shard_map/reduce_sum | solution.py:88
  325.2 3.0 fusion.1
  328.6 3.9 fusion.105
  332.8 14.6 %psum.53 = f32[3,3]{0,1:T(4,128)S(1)} all-reduce(f32[3,3]{0,1:T(4,128)S(1)} %fusion.163), channel_id=1, replica_groups=mesh['bl'=4,'freq'=8] {'freq'}, use_global_device_ids=true, to_apply=%region_27.0 | all-reduce | flops 9 | bytes 72 | tf_op jit(solution)/shard_map/psum | solution.py:227
  351.2 7.7 %reduce-scatter.8.cloned.1.call-done = f32[3,8,16,128]{3,2,1,0:T(8,128)} async-done(((f32[3,8,16,512]{3,2,1,0:T(8,128)}), f32[3,8,16,128]{3,2,1,0:T(8,128)}) %reduce-scatter.8.cloned.1.call-update) | async-done | bytes 196624 | tf_op jit(solution)/shard_map/reduce_scatter | solution.py:206
  360.0 13.2 %all_gather.11 = f32[2,8,16,512]{3,2,1,0:T(8,128)S(1)} all-gather(f32[2,8,16,128]{3,2,1,0:T(8,128)S(1)} %pad_maximum_fusion.9), channel_id=1, replica_groups=mesh['bl'=4,'freq'=8] {'bl'}, dimensions={3}, use_global_device_ids=true | all-gather | bytes 655360 | tf_op jit(solution)/shard_map/all_gather | solution.py:216
  373.2 3.4 fusion
  376.6 3.4 fusion.7
  381.3 2.5 multiply_add_fusion
  383.8 8.9 %fusion.58 = (f32[2,16,2048]{2,1,0:T(8,128)S(1)}, f32[2,16,2048]{2,1,0:T(8,128)S(1)}) fusion(f32[8,16,2048]{2,1,0:T(8,128)S(1)} %bitcast.276, f32[8,16,2048]{2,1,0:T(8,128)S(1)} %bitcast.275, f32[16]{0:T(128)S(1)} %copy-done.28, f32[8,2,2048]{2,1,0:T(2,128)S(1)} %add_multiply_fusion, f32[8,16]{1,0:T(8,128)S(1)} %copy-done.26), kind=kLoop, calls=%fused_computation.68 | loop fusion | flops 5636096 | bytes 2753088 | tf_op jit(solution)/shard_map/reduce_sum | solution.py:60
  393.6 40.2 %all-reduce.3.cloned.1.call-done = f32[3,2,8,512]{3,2,1,0:T(8,128)} async-done(((f32[3,2,8,512]{3,2,1,0:T(8,128)}), f32[3,2,8,512]{3,2,1,0:T(8,128)}) %all-reduce.3.cloned.1.call-update) | async-done | bytes 98320 | tf_op jit(solution)/shard_map/psum | solution.py:227
  433.9 4.0 subtract_divide_fusion
  (127 shorter events, 40.5 us)
Async XLA Ops:
  7.2 85.6 %copy-start = (f32[2,3,8,512]{3,2,1,0:T(8,128)S(1)}, f32[2,3,8,512]{3,2,1,0:T(8,128)}, u32[]{:S(2)}) copy-start(f32[2,3,8,512]{3,2,1,0:T(8,128)} %param.20) | copy-start | bytes 294916
  7.2 111.7 %reduce-scatter.4.cloned.1.call-start = ((), (), s32[]{:S(2)}) async-start(), calls=%async_computation.3 | async-start | bytes 983040 | tf_op jit(solution)/shard_map/reduce_scatter | solution.py:206
  8.0 3.2 copy-start.24
  11.3 2.1 copy-start.29
  13.4 2.6 copy-start.26
  13.5 2.5 copy-start.28
  15.8 9.2 %copy-start.2 = (f32[2,2,16,2048]{3,2,1,0:T(8,128)S(1)}, f32[2,2,16,2048]{3,2,1,0:T(8,128)}, u32[]{:S(2)}) copy-start(f32[2,2,16,2048]{3,2,1,0:T(8,128)} %param.11) | copy-start | bytes 1572868
  16.0 9.8 %copy-start.3 = (s32[2,16,2048]{2,1,0:T(8,128)S(1)}, s32[2,16,2048]{2,1,0:T(8,128)}, u32[]{:S(2)}) copy-start(s32[2,16,2048]{2,1,0:T(8,128)} %param.12) | copy-start | bytes 786436
  72.3 10.9 %copy-start.4 = (f32[128,2048]{1,0:T(8,128)S(1)}, f32[128,2048]{1,0:T(8,128)}, u32[]{:S(2)}) copy-start(f32[128,2048]{1,0:T(8,128)} %get-tuple-element.85) | copy-start | bytes 3145732
  72.3 10.9 %copy-start.5 = (f32[128,2048]{1,0:T(8,128)S(1)}, f32[128,2048]{1,0:T(8,128)}, u32[]{:S(2)}) copy-start(f32[128,2048]{1,0:T(8,128)} %get-tuple-element.86) | copy-start | bytes 3145732
  72.3 10.9 %copy-start.6 = (f32[128,2048]{1,0:T(8,128)S(1)}, f32[128,2048]{1,0:T(8,128)}, u32[]{:S(2)}) copy-start(f32[128,2048]{1,0:T(8,128)} %get-tuple-element.87) | copy-start | bytes 3145732
  72.3 10.9 %copy-start.7 = (f32[128,2048]{1,0:T(8,128)S(1)}, f32[128,2048]{1,0:T(8,128)}, u32[]{:S(2)}) copy-start(f32[128,2048]{1,0:T(8,128)} %get-tuple-element.88) | copy-start | bytes 3145732
  88.6 4.0 copy-start.30
  88.6 4.1 copy-start.25
  92.6 146.1 %reduce-scatter.6.cloned.1.call-start = ((), (), s32[]{:S(2)}) async-start(), calls=%async_computation.4 | async-start | bytes 983040 | tf_op jit(solution)/shard_map/reduce_scatter | solution.py:206
  94.4 40.8 %copy-start.22 = (f32[1,8,16,512]{3,2,1,0:T(8,128)}, f32[1,8,16,512]{3,2,1,0:T(8,128)S(1)}, u32[]{:S(2)}) copy-start(f32[1,8,16,512]{3,2,1,0:T(8,128)S(1)} %get-tuple-element.99) | copy-start | bytes 786436
  94.4 40.8 %copy-start.23 = (f32[1,8,16,512]{3,2,1,0:T(8,128)}, f32[1,8,16,512]{3,2,1,0:T(8,128)S(1)}, u32[]{:S(2)}) copy-start(f32[1,8,16,512]{3,2,1,0:T(8,128)S(1)} %get-tuple-element.100) | copy-start | bytes 786436
  133.1 2.1 copy-start.20
  192.3 10.9 %copy-start.12 = (f32[128,2048]{1,0:T(8,128)S(1)}, f32[128,2048]{1,0:T(8,128)}, u32[]{:S(2)}) copy-start(f32[128,2048]{1,0:T(8,128)} %get-tuple-element.77) | copy-start | bytes 3145732
  192.3 10.9 %copy-start.13 = (f32[128,2048]{1,0:T(8,128)S(1)}, f32[128,2048]{1,0:T(8,128)}, u32[]{:S(2)}) copy-start(f32[128,2048]{1,0:T(8,128)} %get-tuple-element.78) | copy-start | bytes 3145732
  192.4 10.9 %copy-start.14 = (f32[128,2048]{1,0:T(8,128)S(1)}, f32[128,2048]{1,0:T(8,128)}, u32[]{:S(2)}) copy-start(f32[128,2048]{1,0:T(8,128)} %get-tuple-element.79) | copy-start | bytes 3145732
  192.4 10.9 %copy-start.15 = (f32[128,2048]{1,0:T(8,128)S(1)}, f32[128,2048]{1,0:T(8,128)}, u32[]{:S(2)}) copy-start(f32[128,2048]{1,0:T(8,128)} %get-tuple-element.80) | copy-start | bytes 3145732
  208.4 4.0 copy-start.21
  212.4 146.5 %reduce-scatter.8.cloned.1.call-start = ((), (), s32[]{:S(2)}) async-start(), calls=%async_computation.5 | async-start | bytes 983040 | tf_op jit(solution)/shard_map/reduce_scatter | solution.py:206
  312.5 10.9 %copy-start.8 = (f32[128,2048]{1,0:T(8,128)S(1)}, f32[128,2048]{1,0:T(8,128)}, u32[]{:S(2)}) copy-start(f32[128,2048]{1,0:T(8,128)} %get-tuple-element.69) | copy-start | bytes 3145732
  312.5 10.9 %copy-start.9 = (f32[128,2048]{1,0:T(8,128)S(1)}, f32[128,2048]{1,0:T(8,128)}, u32[]{:S(2)}) copy-start(f32[128,2048]{1,0:T(8,128)} %get-tuple-element.70) | copy-start | bytes 3145732
  312.5 10.9 %copy-start.10 = (f32[128,2048]{1,0:T(8,128)S(1)}, f32[128,2048]{1,0:T(8,128)}, u32[]{:S(2)}) copy-start(f32[128,2048]{1,0:T(8,128)} %get-tuple-element.71) | copy-start | bytes 3145732
  312.6 10.9 %copy-start.11 = (f32[128,2048]{1,0:T(8,128)S(1)}, f32[128,2048]{1,0:T(8,128)}, u32[]{:S(2)}) copy-start(f32[128,2048]{1,0:T(8,128)} %get-tuple-element.72) | copy-start | bytes 3145732
  328.6 22.5 %copy-start.19 = (f32[2,8,16,512]{3,2,1,0:T(8,128)S(1)}, f32[2,8,16,512]{3,2,1,0:T(8,128)}, u32[]{:S(2)}) copy-start(f32[2,8,16,512]{3,2,1,0:T(8,128)} %copy-done.18) | copy-start | bytes 1572868
  332.6 101.3 %all-reduce.3.cloned.1.call-start = ((), (), s32[]{:S(2)}) async-start(), calls=%async_computation.6 | async-start | bytes 196608 | tf_op jit(solution)/shard_map/psum | solution.py:227
  376.6 3.5 copy-start.17
  392.7 48.1 %copy-start.1 = (f32[2,3,8,512]{3,2,1,0:T(8,128)S(1)}, f32[2,3,8,512]{3,2,1,0:T(8,128)}, u32[]{:S(2)}) copy-start(f32[2,3,8,512]{3,2,1,0:T(8,128)} %param.20) | copy-start | bytes 294916
  (3 other events, 5.3 us)
Sparse Core Ops, SparseCore 0:
  92.7 26.1 reduce-scatter.3
  212.5 26.1 reduce-scatter.5
  332.7 26.1 reduce-scatter.7
  381.4 52.4 all-reduce.2
where the time goes:
time: 453 us; the launch traced here: 448 us
  blocking collectives  177 us (39%)
  other arithmetic  104 us (23%)
  waiting for transfers between devices  98.6 us (22%)
  matrix products  44.3 us (10%)
  between operations  18.7 us (4%)
  local copies, waits for them, and re-layouts  4.85 us (1%)
    psum x3, blocking collectives, body(): lax.psum((misfit_local, count_local), ('bl', 'freq'))  122 us
    reduce_scatter x3, waiting for transfers between devices, body(): lax.psum_scatter(partial_value, 'bl', scatter_dimension=3, tiled=True)  58.3 us
    psum x1, waiting for transfers between devices, body(): rhs_total, gram_total = lax.psum((rhs_local, gram_local), 'freq')  40.2 us
    all_gather x3, blocking collectives, body(): lax.all_gather(jnp.stack([new_re, new_im]), 'bl', axis=3, tiled=True)  39.7 us
    reduce_sum x4, other arithmetic, residual_of(): jnp.sum(model_re, axis=0)  35.9 us
    reduce_sum x3, other arithmetic, normal_terms(): summed_re = jnp.sum(weight_wide * cross_re, axis=1)  32.6 us
    dot_general x8, matrix products, pick_stations(): jnp.dot(flat, table, precision=lax.Precision.HIGHEST, preferred_element_t...  20.6 us
    psum x1, blocking collectives, body(): rhs_total, gram_total = lax.psum((rhs_local, gram_local), 'freq')  14.6 us
  transfers between devices with their start and end apart: 4, of which 4 were waited for; matrix products, arithmetic and copies ran while one was open for 4% of the time, Pallas kernels for 0%

commit v1 on v0

v1 whole, which is shorter than its diff:
```python
import functools
import math

import jax
import jax.numpy as jnp
from jax import lax
from jax.experimental import pallas as pl
from jax.experimental.pallas import tpu as pltpu
from jax.sharding import PartitionSpec as P

NPOLY = 3
ITERS = 3

robust_dof = 2.0
small_term = 1e-06
two_pi = 2.0 * math.pi
MESH = pl.DeviceIdType.MESH

SIN_TERMS = [(-1.0) ** n * two_pi ** (2 * n + 1) / math.factorial(2 * n + 1) for n in range(6)]
COS_TERMS = [(-1.0) ** n * two_pi ** (2 * n) / math.factorial(2 * n) for n in range(7)]


def horner(terms, square):
    value = jnp.full_like(square, terms[-1])
    for term in terms[-2::-1]:
        value = value * square + term
    return value


def turn_parts(turns):
    half = jnp.floor(turns * 2.0 + 0.5)
    rest = turns - half * 0.5
    sign = 1.0 - 2.0 * (half - 2.0 * jnp.floor(half * 0.5))
    square = rest * rest
    return horner(COS_TERMS, square), rest * horner(SIN_TERMS, square), sign


def column(row, count):
    spread = jnp.broadcast_to(row, (count, count))
    r = lax.broadcasted_iota(jnp.int32, (count, count), 0)
    c = lax.broadcasted_iota(jnp.int32, (count, count), 1)
    return jnp.sum(jnp.where(r == c, spread, 0.0), axis=1, keepdims=True)


def split_two(value):
    high = value.astype(jnp.bfloat16)
    low = (value - high.astype(jnp.float32)).astype(jnp.bfloat16)
    return high, low


def kernel(
    sizes,
    vis,
    flag,
    pair,
    coords,
    dirs,
    flux,
    ratio,
    gains_in,
    dual,
    cons_in,
    penalty,
    gains_out,
    cons_out,
    dual_out,
    resid_out,
    table,
    sky,
    side,
    gsplit,
    err,
    weighted,
    wsum,
    flux_sq,
    stacked,
    partial,
    rs_buf,
    gains,
    s_bl,
    s_fr,
    c_fr,
    c_bl,
    rs_send,
    rs_recv,
    ag_send,
    ag_recv,
    sb_send,
    sb_recv,
    sf_send,
    sf_recv,
    cf_send,
    cf_recv,
    cb_send,
    cb_recv,
):
    nb, nf, slots, chans, base, dirn, stations, ch, rho_scale = sizes
    kb = dirn // nb
    chunks = base // ch
    me = lax.axis_index("bl")
    mf = lax.axis_index("freq")
    own = me * kb

    barrier = pltpu.get_barrier_semaphore()
    for o in range(1, nb):
        pl.semaphore_signal(
            barrier, inc=1, device_id={"bl": lax.rem(me + o, nb)}, device_id_type=MESH
        )
    for o in range(1, nf):
        pl.semaphore_signal(
            barrier, inc=1, device_id={"freq": lax.rem(mf + o, nf)}, device_id_type=MESH
        )

    def remote(src, dst, send, recv, axis, target):
        return pltpu.make_async_remote_copy(
            src_ref=src,
            dst_ref=dst,
            send_sem=send,
            recv_sem=recv,
            device_id={axis: target},
            device_id_type=MESH,
        )

    ratio_col = column(ratio[...], chans)
    scaled = (ratio_col - 1.05) / 0.35
    basis = [jnp.ones_like(scaled), scaled, (3.0 * scaled * scaled - 1.0) / 2.0]
    flux_cols = [column(flux[k : k + 1, :], chans) for k in range(dirn)]
    for k in range(dirn):
        flux_sq[k] = jnp.broadcast_to(flux_cols[k] * flux_cols[k], (chans, ch))

    def setup(i, count):
        at = pl.multiple_of(i * ch, ch)
        cols = pl.ds(at, ch)
        rows = lax.broadcasted_iota(jnp.int32, (stations, ch), 0)
        for s in range(2):
            hit = rows == pair[s : s + 1, cols]
            table[:, pl.ds(pl.multiple_of(s * base + at, ch), ch)] = jnp.where(
                hit, 1.0, 0.0
            ).astype(jnp.bfloat16)
        for t in range(slots):
            u = coords[0, t : t + 1, cols]
            v = coords[1, t : t + 1, cols]
            for k in range(dirn):
                project = dirs[0, k] * u + dirs[1, k] * v
                cosine, sine, sign = turn_parts(project * ratio_col)
                amplitude = sign * flux_cols[k]
                sky[0, k, t, :, cols] = amplitude * cosine
                sky[1, k, t, :, cols] = amplitude * sine
            count = count + tile_sum(flag[t, :, cols].astype(jnp.float32))
        return count

    def tile_sum(value):
        total = value[:8]
        for r in range(8, chans, 8):
            total = total + value[r : r + 8]
        out = total[:, :128]
        for c in range(128, ch, 128):
            out = out + total[:, c : c + 128]
        return out

    count = lax.fori_loop(0, chunks, setup, jnp.zeros((8, 128), jnp.float32))
    for it in range(ITERS):
        s_bl[it, me, 1] = count
    gains[0] = gains_in[...]

    pl.semaphore_wait(barrier, nb + nf - 2)

    def predict(it, target):
        high, low = split_two(gains[it].reshape(2 * dirn * chans, stations))
        gsplit[0] = high
        gsplit[1] = low

        def step(i, misfit):
            at = pl.multiple_of(i * ch, ch)
            cols = pl.ds(at, ch)
            left = gsplit[...].reshape(2 * 2 * dirn * chans, stations)
            half = 2 * dirn * chans
            for s in range(2):
                where = pl.ds(pl.multiple_of(s * base + at, ch), ch)
                both = jnp.dot(left, table[:, where], preferred_element_type=jnp.float32)
                side[:, :, :, where] = (both[:half] + both[half:]).reshape(2, dirn, chans, ch)
            right = pl.ds(pl.multiple_of(base + at, ch), ch)
            er = [vis[0, t, :, cols] for t in range(slots)]
            ei = [vis[1, t, :, cols] for t in range(slots)]
            for k in range(dirn):
                lr, li = side[0, k, :, cols], side[1, k, :, cols]
                rr, ri = side[0, k, :, right], side[1, k, :, right]
                pr = lr * rr + li * ri
                pi = li * rr - lr * ri
                for t in range(slots):
                    sr, si = sky[0, k, t, :, cols], sky[1, k, t, :, cols]
                    er[t] = er[t] - (pr * sr - pi * si)
                    ei[t] = ei[t] - (pr * si + pi * sr)
            for t in range(slots):
                target[0, t, :, cols] = er[t]
                target[1, t, :, cols] = ei[t]
                power = er[t] * er[t] + ei[t] * ei[t]
                misfit = misfit + tile_sum(flag[t, :, cols].astype(jnp.float32) * power)
            return misfit

        return lax.fori_loop(0, chunks, step, jnp.zeros((8, 128), jnp.float32))

    def iteration(it, carry):
        s_bl[it, me, 0] = predict(it, err)
        copies = [
            remote(
                s_bl.at[it, me], s_bl.at[it, me], sb_send.at[it, o], sb_recv.at[it, o],
                "bl", lax.rem(me + o, nb),
            )
            for o in range(1, nb)
        ]
        for copy in copies:
            copy.start()
        for copy in copies:
            copy.wait_recv()
        total = s_bl[it, 0]
        for o in range(1, nb):
            total = total + s_bl[it, o]
        s_fr[it, mf] = total
        more = [
            remote(
                s_fr.at[it, mf], s_fr.at[it, mf], sf_send.at[it, o], sf_recv.at[it, o],
                "freq", lax.rem(mf + o, nf),
            )
            for o in range(1, nf)
        ]
        for copy in more:
            copy.start()
        for copy in more:
            copy.wait_recv()
        total = s_fr[it, 0]
        for o in range(1, nf):
            total = total + s_fr[it, o]
        lanes = jnp.sum(total, axis=2, keepdims=True)
        sums = jnp.sum(lanes, axis=1, keepdims=True)
        sigma_sq = sums[0] / (sums[1] + 1.0) + small_term
        inverse = 1.0 / sigma_sq

        def weigh(i, carry):
            cols = pl.ds(pl.multiple_of(i * ch, ch), ch)
            total = None
            for t in range(slots):
                er, ei = err[0, t, :, cols], err[1, t, :, cols]
                power = er * er + ei * ei
                r = (
                    flag[t, :, cols].astype(jnp.float32)
                    * (robust_dof + 1.0)
                    / (robust_dof + power * inverse)
                )
                weighted[0, t, :, cols] = r * er
                weighted[1, t, :, cols] = r * ei
                total = r if total is None else total + r
            wsum[:, cols] = total
            return carry

        lax.fori_loop(0, chunks, weigh, 0)

        sends = []
        for o in list(range(1, nb)) + [0]:
            owner = lax.rem(me + o, nb)
            first = owner * kb

            def normal(i, carry, first=first):
                at = pl.multiple_of(i * ch, ch)
                cols = pl.ds(at, ch)
                right = pl.ds(pl.multiple_of(base + at, ch), ch)
                for kk in range(kb):
                    k = first + kk
                    lr, li = side[0, k, :, cols], side[1, k, :, cols]
                    rr, ri = side[0, k, :, right], side[1, k, :, right]
                    c2 = flux_sq[k] * wsum[:, cols]
                    xr = (lr * rr + li * ri) * c2
                    xi = (li * rr - lr * ri) * c2
                    for t in range(slots):
                        sr, si = sky[0, k, t, :, cols], sky[1, k, t, :, cols]
                        wr, wi = weighted[0, t, :, cols], weighted[1, t, :, cols]
                        xr = xr + (sr * wr + si * wi)
                        xi = xi + (sr * wi - si * wr)
                    terms = (
                        (rr * xr - ri * xi, lr * xr + li * xi),
                        (rr * xi + ri * xr, li * xr - lr * xi),
                        ((rr * rr + ri * ri) * c2, (lr * lr + li * li) * c2),
                    )
                    for q in range(3):
                        for s, where in enumerate((cols, right)):
                            high, low = split_two(terms[q][s])
                            stacked[0, q, kk, :, where] = high
                            stacked[1, q, kk, :, where] = low
                return carry

            lax.fori_loop(0, chunks, normal, 0)
            half = 3 * kb * chans
            both = lax.dot_general(
                stacked[...].reshape(2 * half, 2 * base),
                table[...],
                (((1,), (1,)), ((), ())),
                preferred_element_type=jnp.float32,
            )
            partial[it, o] = (both[:half] + both[half:]).reshape(3, kb, chans, stations)
            if o > 0:
                copy = remote(
                    partial.at[it, o], rs_buf.at[it, o], rs_send.at[it, o], rs_recv.at[it, o],
                    "bl", owner,
                )
                copy.start()
                sends.append(copy)
        for copy in sends:
            copy.wait_recv()

        for kk in range(kb):
            k = own + kk
            rho = penalty[k] * rho_scale
            sums_k = []
            for q in range(3):
                value = partial[it, 0, q, kk]
                for o in range(1, nb):
                    value = value + rs_buf[it, o, q, kk]
                sums_k.append(value)
            divisor = 1.0 / (sums_k[2] + rho)
            for c in range(2):
                anchor = -dual[c, k]
                for j in range(NPOLY):
                    anchor = anchor + basis[j] * cons_in[c, j, pl.ds(k, 1), :]
                solved = (sums_k[c] + rho * anchor) * divisor
                gains[it + 1, c, k] = 0.5 * (gains[it, c, k] + solved)
        block = gains.at[it + 1, :, pl.ds(own, kb)]
        spread = [
            remote(
                block, block, ag_send.at[it, o], ag_recv.at[it, o], "bl", lax.rem(me + o, nb)
            )
            for o in range(1, nb)
        ]
        for copy in spread:
            copy.start()
        for copy in spread:
            copy.wait_recv()
        for copy in copies + more + sends + spread:
            copy.wait_send()
        return carry

    lax.fori_loop(0, ITERS, iteration, 0)

    rows = 2 * NPOLY * kb
    for c in range(2):
        for kk in range(kb):
            both = gains[ITERS, c, own + kk] + dual[c, own + kk]
            for j in range(NPOLY):
                row = (c * NPOLY + j) * kb + kk
                c_fr[mf, row : row + 1, :] = jnp.sum(basis[j] * both, axis=0, keepdims=True)
    grams = [(a, b) for a in range(NPOLY) for b in range(a + 1)]
    for n, (a, b) in enumerate(grams):
        entry = jnp.sum(basis[a] * basis[b], axis=0, keepdims=True)
        c_fr[mf, rows + n : rows + n + 1, :] = jnp.broadcast_to(entry, (1, stations))
    for row in range(rows + len(grams), c_fr.shape[1]):
        c_fr[mf, row : row + 1, :] = jnp.zeros((1, stations), jnp.float32)
    more = [
        remote(
            c_fr.at[mf], c_fr.at[mf], cf_send.at[o], cf_recv.at[o], "freq", lax.rem(mf + o, nf)
        )
        for o in range(1, nf)
    ]
    for copy in more:
        copy.start()

    predict(ITERS, resid_out)
    gains_out[...] = gains[ITERS]

    for copy in more:
        copy.wait_recv()
    total = c_fr[0]
    for o in range(1, nf):
        total = total + c_fr[o]
    gram = {ab: total[rows + n : rows + n + 1] for n, ab in enumerate(grams)}
    factor = {}
    for a in range(NPOLY):
        for b in range(a + 1):
            value = gram[a, b]
            for m in range(b):
                value = value - factor[a, m] * factor[b, m]
            factor[a, b] = jnp.sqrt(value) if a == b else value / factor[b, b]
    for c in range(2):
        part = [
            total[(c * NPOLY + j) * kb : (c * NPOLY + j + 1) * kb] for j in range(NPOLY)
        ]
        forward = []
        for a in range(NPOLY):
            running = part[a]
            for b in range(a):
                running = running - factor[a, b] * forward[b]
            forward.append(running / factor[a, a])
        backward = [None] * NPOLY
        for a in reversed(range(NPOLY)):
            running = forward[a]
            for b in range(a + 1, NPOLY):
                running = running - factor[b, a] * backward[b]
            backward[a] = running / factor[a, a]
        for j in range(NPOLY):
            row = (c * NPOLY + j) * kb
            c_bl[me, row : row + kb, :] = backward[j]
    for row in range(rows, c_bl.shape[1]):
        c_bl[me, row : row + 1, :] = jnp.zeros((1, stations), jnp.float32)
    spread = [
        remote(
            c_bl.at[me], c_bl.at[me], cb_send.at[o], cb_recv.at[o], "bl", lax.rem(me + o, nb)
        )
        for o in range(1, nb)
    ]
    for copy in spread:
        copy.start()
    for copy in spread:
        copy.wait_recv()
    for g in range(nb):
        for kk in range(kb):
            k = g * kb + kk
            for c in range(2):
                value = dual[c, k] + gains[ITERS, c, k]
                for j in range(NPOLY):
                    row = (c * NPOLY + j) * kb + kk
                    coefficient = c_bl[g, row : row + 1, :]
                    cons_out[c, j, k : k + 1, :] = coefficient
                    value = value - basis[j] * coefficient
                dual_out[c, k] = value
    for copy in more + spread:
        copy.wait_send()


def body(nb, nf, vis, flag, pair, coords, dirs, flux, ratio, gains, dual, cons, penalty):
    f32, bf16 = jnp.float32, jnp.bfloat16
    _, slots, chans, base = vis.shape
    dirn, stations = gains.shape[1], gains.shape[3]
    kb = dirn // nb
    ch = 256
    rho_scale = 2.0 * base * nb * slots / stations
    sizes = (nb, nf, slots, chans, base, dirn, stations, ch, rho_scale)
    pad = lambda n: -(-n // 8) * 8
    rows = 2 * NPOLY * kb
    vmem = pl.BlockSpec(memory_space=pltpu.VMEM)
    smem = pl.BlockSpec(memory_space=pltpu.SMEM)
    dma = pltpu.SemaphoreType.DMA
    shape = jax.ShapeDtypeStruct
    return pl.pallas_call(
        functools.partial(kernel, sizes),
        name="admm_step",
        out_shape=(
            shape(gains.shape, f32),
            shape(cons.shape, f32),
            shape(dual.shape, f32),
            shape(vis.shape, f32),
        ),
        in_specs=[vmem, vmem, vmem, vmem, smem, vmem, vmem, vmem, vmem, vmem, smem],
        out_specs=(vmem, vmem, vmem, vmem),
        scratch_shapes=[
            pltpu.VMEM((stations, 2 * base), bf16),
            pltpu.VMEM((2, dirn, slots, chans, base), f32),
            pltpu.VMEM((2, dirn, chans, 2 * base), f32),
            pltpu.VMEM((2, 2 * dirn * chans, stations), bf16),
            pltpu.VMEM((2, slots, chans, base), f32),
            pltpu.VMEM((2, slots, chans, base), f32),
            pltpu.VMEM((chans, base), f32),
            pltpu.VMEM((dirn, chans, ch), f32),
            pltpu.VMEM((2, 3, kb, chans, 2 * base), bf16),
            pltpu.VMEM((ITERS, nb, 3, kb, chans, stations), f32),
            pltpu.VMEM((ITERS, nb, 3, kb, chans, stations), f32),
            pltpu.VMEM((ITERS + 1,) + gains.shape, f32),
            pltpu.VMEM((ITERS, nb, 2, 8, 128), f32),
            pltpu.VMEM((ITERS, nf, 2, 8, 128), f32),
            pltpu.VMEM((nf, pad(rows + 6), stations), f32),
            pltpu.VMEM((nb, pad(rows), stations), f32),
            dma((ITERS, nb)),
            dma((ITERS, nb)),
            dma((ITERS, nb)),
            dma((ITERS, nb)),
            dma((ITERS, nb)),
            dma((ITERS, nb)),
            dma((ITERS, nf)),
            dma((ITERS, nf)),
            dma((nf,)),
            dma((nf,)),
            dma((nb,)),
            dma((nb,)),
        ],
        compiler_params=pltpu.CompilerParams(
            collective_id=0, has_side_effects=True, vmem_limit_bytes=60 * 1024 * 1024
        ),
    )(vis, flag, pair, coords, dirs, flux, ratio.reshape(1, -1), gains, dual, cons, penalty)


def solution(mesh):
    in_specs = (
        P(None, None, "freq", "bl"),
        P(None, "freq", "bl"),
        P(None, "bl"),
        P(None, None, "bl"),
        P(),
        P(None, "freq"),
        P("freq"),
        P(None, None, "freq", None),
        P(None, None, "freq", None),
        P(),
        P(),
    )
    out_specs = (
        P(None, None, "freq", None),
        P(),
        P(None, None, "freq", None),
        P(None, None, "freq", "bl"),
    )
    step = functools.partial(body, mesh.shape["bl"], mesh.shape["freq"])
    return jax.shard_map(step, mesh=mesh, in_specs=in_specs, out_specs=out_specs, check_vma=False)
```

time: 453 us -> 129 us (0.28); the launches traced: 448 us -> 129 us
  blocking collectives: 177 us -> 0 us
  Pallas kernels: 0 us -> 124 us
  other arithmetic: 104 us -> 0 us
  waiting for transfers between devices: 98.6 us -> 0 us
  matrix products: 44.3 us -> 0 us
  between operations: 18.7 us -> 0.66 us
    psum x4 -> x0, blocking collectives: 137 us -> none  [the longest x3 122 us: body(): lax.psum((misfit_local, count_local), ('bl', 'freq'))]
    pallas_call x0 -> x1, Pallas kernels: none -> 124 us  [body(): pl.pallas_call(functools.partial(kernel, sizes), name='admm_step', out_sh...]
    reduce_sum x10 -> x0, other arithmetic: 72.7 us -> none  [the longest x4 35.9 us: residual_of(): jnp.sum(model_re, axis=0)]
    reduce_scatter x3 -> x0, waiting for transfers between devices: 58.3 us -> none  [body(): lax.psum_scatter(partial_value, 'bl', scatter_dimension=3, tiled=True)]
    dot_general x18 -> x0, matrix products: 44.3 us -> none  [the longest x8 20.6 us: pick_stations(): jnp.dot(flat, table, precision=lax.Precision.HIGHEST, preferred_element_t...]
    psum x1 -> x0, waiting for transfers between devices: 40.2 us -> none  [body(): rhs_total, gram_total = lax.psum((rhs_local, gram_local), 'freq')]
    all_gather x3 -> x0, blocking collectives: 39.7 us -> none  [body(): lax.all_gather(jnp.stack([new_re, new_im]), 'bl', axis=3, tiled=True)]
    add x11 -> x0, other arithmetic: 16.7 us -> none  [the longest x4 9.64 us: predict(): pair_re = left_re * right_re + left_im * right_im]
  transfers between devices with their start and end apart: 4 -> 0, of which waited for: 4 -> 0; matrix products, arithmetic and copies ran while one was open for 4% -> 0% of each run, Pallas kernels for 0% -> 0%
where the time goes in v1:
time: 129 us
  Pallas kernels  124 us (96%)
  local copies, waits for them, and re-layouts  4.62 us (4%)
    pallas_call x1, Pallas kernels, body(): pl.pallas_call(functools.partial(kernel, sizes), name='admm_step', out_sh...  124 us
    unnamed x10, local copies, waits for them, and re-layouts  4.62 us

profile of v1, /device:TPU:0, one launch (start us, length us, event | category | flops | bytes accessed | tf_op | source)
XLA Modules:
  0.0 129.0 jit_solution(3219427877556050534)
XLA Ops:
  0.6 123.8 %admm_step.1 = (f32[2,8,16,512]{3,2,1,0:T(8,128)}, f32[2,3,8,512]{3,2,1,0:T(8,128)}, f32[2,8,16,512]{3,2,1,0:T(8,128)}, f32[2,2,16,2048]{3,2,1,0:T(8,128)}) custom-call(f32[2,2,16,2048]{3,2,1,0:T(8,128)} %vis.1, s32[2,16,2048]{2,1,0:T(8,128)} %flag.1, s32[2,2048]{1,0:T(2,128)} %pair.1, f32[2,2,2048]{2,1,0:T(2,128)} %coords.1, f32[2,8]{1,0:T(2,128)} %dirs.1, ...), custom_call_target="tpu_custom_call" | custom-call | tf_op jit(solution)/shard_map/admm_step/pallas_call | solution.py:441
  124.4 0.0 copy-start.2
  124.4 0.0 copy-start.1
  124.4 1.9 %copy.19 = f32[2,8,16,512]{3,2,1,0:T(8,128)} copy(f32[2,8,16,512]{3,2,1,0:T(8,128)} %get-tuple-element.8) | data formatting | bytes 1048576
  126.4 0.0 copy-done.2
  126.4 0.6 copy.20
  127.0 0.0 copy-done.1
  127.0 0.0 copy-start
  127.0 0.8 copy.21
  127.8 0.4 copy-done
  128.2 0.8 copy.22
Async XLA Ops:
  124.4 2.0 %copy-start.2 = (f32[2,3,8,512]{3,2,1,0:T(8,128)S(1)}, f32[2,3,8,512]{3,2,1,0:T(8,128)}, u32[]{:S(2)}) copy-start(f32[2,3,8,512]{3,2,1,0:T(8,128)} %get-tuple-element.9) | copy-start | bytes 294916
  124.4 2.6 %copy-start.1 = (f32[2,8,16,512]{3,2,1,0:T(8,128)S(1)}, f32[2,8,16,512]{3,2,1,0:T(8,128)}, u32[]{:S(2)}) copy-start(f32[2,8,16,512]{3,2,1,0:T(8,128)} %get-tuple-element.10) | copy-start | bytes 1572868
  127.0 1.2 copy-start

commit v2 on v1

--- a/solution.py
+++ b/solution.py
@@ -101,10 +101,13 @@
     mf = lax.axis_index("freq")
     own = me * kb
 
+    def bl_peer(o):
+        return lax.bitwise_xor(me, o)
+
     barrier = pltpu.get_barrier_semaphore()
     for o in range(1, nb):
         pl.semaphore_signal(
-            barrier, inc=1, device_id={"bl": lax.rem(me + o, nb)}, device_id_type=MESH
+            barrier, inc=1, device_id={"bl": bl_peer(o)}, device_id_type=MESH
         )
     for o in range(1, nf):
         pl.semaphore_signal(
@@ -165,47 +168,62 @@
 
     pl.semaphore_wait(barrier, nb + nf - 2)
 
-    def predict(it, target):
-        high, low = split_two(gains[it].reshape(2 * dirn * chans, stations))
-        gsplit[0] = high
-        gsplit[1] = low
-
-        def step(i, misfit):
-            at = pl.multiple_of(i * ch, ch)
-            cols = pl.ds(at, ch)
-            left = gsplit[...].reshape(2 * 2 * dirn * chans, stations)
-            half = 2 * dirn * chans
-            for s in range(2):
-                where = pl.ds(pl.multiple_of(s * base + at, ch), ch)
-                both = jnp.dot(left, table[:, where], preferred_element_type=jnp.float32)
-                side[:, :, :, where] = (both[:half] + both[half:]).reshape(2, dirn, chans, ch)
-            right = pl.ds(pl.multiple_of(base + at, ch), ch)
-            er = [vis[0, t, :, cols] for t in range(slots)]
-            ei = [vis[1, t, :, cols] for t in range(slots)]
-            for k in range(dirn):
-                lr, li = side[0, k, :, cols], side[1, k, :, cols]
-                rr, ri = side[0, k, :, right], side[1, k, :, right]
-                pr = lr * rr + li * ri
-                pi = li * rr - lr * ri
+    def predict(it, target, arrivals):
+        half = 2 * kb * chans
+        misfit = jnp.zeros((8, 128), jnp.float32)
+        for o in range(nb):
+            if o > 0 and arrivals is not None:
+                arrivals(o).wait_recv()
+            first = bl_peer(o) * kb
+            block = gains[it, :, pl.ds(first, kb)].reshape(half, stations)
+            high, low = split_two(block)
+            gsplit[o, 0] = high
+            gsplit[o, 1] = low
+
+            def step(i, misfit, o=o, first=first):
+                at = pl.multiple_of(i * ch, ch)
+                cols = pl.ds(at, ch)
+                left = gsplit[o].reshape(2 * half, stations)
+                right = pl.ds(pl.multiple_of(base + at, ch), ch)
+                found = []
+                for where in (cols, right):
+                    both = jnp.dot(left, table[:, where], preferred_element_type=jnp.float32)
+                    found.append((both[:half] + both[half:]).reshape(2, kb, chans, ch))
+                    side[:, pl.ds(first, kb), :, where] = found[-1]
+                source = vis if o == 0 else target
+                er = [source[0, t, :, cols] for t in range(slots)]
+                ei = [source[1, t, :, cols] for t in range(slots)]
+                for kk in range(kb):
+                    lr, li = found[0][0, kk], found[0][1, kk]
+                    rr, ri = found[1][0, kk], found[1][1, kk]
+                    pr = lr * rr + li * ri
+                    pi = li * rr - lr * ri
+                    for t in range(slots):
+                        k = first + kk
+                        sr, si = sky[0, k, t, :, cols], sky[1, k, t, :, cols]
+                        er[t] = er[t] - (pr * sr - pi * si)
+                        ei[t] = ei[t] - (pr * si + pi * sr)
                 for t in range(slots):
-                    sr, si = sky[0, k, t, :, cols], sky[1, k, t, :, cols]
-                    er[t] = er[t] - (pr * sr - pi * si)
-                    ei[t] = ei[t] - (pr * si + pi * sr)
-            for t in range(slots):
-                target[0, t, :, cols] = er[t]
-                target[1, t, :, cols] = ei[t]
-                power = er[t] * er[t] + ei[t] * ei[t]
-                misfit = misfit + tile_sum(flag[t, :, cols].astype(jnp.float32) * power)
-            return misfit
-
-        return lax.fori_loop(0, chunks, step, jnp.zeros((8, 128), jnp.float32))
-
-    def iteration(it, carry):
-        s_bl[it, me, 0] = predict(it, err)
+                    target[0, t, :, cols] = er[t]
+                    target[1, t, :, cols] = ei[t]
+                    if o == nb - 1:
+                        power = er[t] * er[t] + ei[t] * ei[t]
+                        misfit = misfit + tile_sum(flag[t, :, cols].astype(jnp.float32) * power)
+                return misfit
+
+            misfit = lax.fori_loop(0, chunks, step, misfit)
+        return misfit
+
+    def gather_copy(it, o):
+        block = gains.at[it, :, pl.ds(own, kb)]
+        return remote(block, block, ag_send.at[it - 1, o], ag_recv.at[it - 1, o], "bl", bl_peer(o))
+
+    def iteration(it, misfit, target=err, rhs_hook=None):
+        s_bl[it, me, 0] = misfit
         copies = [
             remote(
                 s_bl.at[it, me], s_bl.at[it, me], sb_send.at[it, o], sb_recv.at[it, o],
-                "bl", lax.rem(me + o, nb),
+                "bl", bl_peer(o),
             )
             for o in range(1, nb)
         ]
@@ -256,8 +274,8 @@
         lax.fori_loop(0, chunks, weigh, 0)
 
         sends = []
-        for o in list(range(1, nb)) + [0]:
-            owner = lax.rem(me + o, nb)
+        for o in reversed(range(nb)):
+            owner = bl_peer(o)
             first = owner * kb
 
             def normal(i, carry, first=first):
@@ -323,46 +341,42 @@
                     anchor = anchor + basis[j] * cons_in[c, j, pl.ds(k, 1), :]
                 solved = (sums_k[c] + rho * anchor) * divisor
                 gains[it + 1, c, k] = 0.5 * (gains[it, c, k] + solved)
-        block = gains.at[it + 1, :, pl.ds(own, kb)]
-        spread = [
-            remote(
-                block, block, ag_send.at[it, o], ag_recv.at[it, o], "bl", lax.rem(me + o, nb)
-            )
-            for o in range(1, nb)
-        ]
+        spread = [gather_copy(it + 1, o) for o in range(1, nb)]
         for copy in spread:
             copy.start()
-        for copy in spread:
-            copy.wait_recv()
+        if rhs_hook is not None:
+            rhs_hook()
+        result = predict(it + 1, target, lambda o: gather_copy(it + 1, o))
         for copy in copies + more + sends + spread:
             copy.wait_send()
-        return carry
-
-    lax.fori_loop(0, ITERS, iteration, 0)
+        return result
 
     rows = 2 * NPOLY * kb
-    for c in range(2):
-        for kk in range(kb):
-            both = gains[ITERS, c, own + kk] + dual[c, own + kk]
-            for j in range(NPOLY):
-                row = (c * NPOLY + j) * kb + kk
-                c_fr[mf, row : row + 1, :] = jnp.sum(basis[j] * both, axis=0, keepdims=True)
     grams = [(a, b) for a in range(NPOLY) for b in range(a + 1)]
-    for n, (a, b) in enumerate(grams):
-        entry = jnp.sum(basis[a] * basis[b], axis=0, keepdims=True)
-        c_fr[mf, rows + n : rows + n + 1, :] = jnp.broadcast_to(entry, (1, stations))
-    for row in range(rows + len(grams), c_fr.shape[1]):
-        c_fr[mf, row : row + 1, :] = jnp.zeros((1, stations), jnp.float32)
     more = [
         remote(
             c_fr.at[mf], c_fr.at[mf], cf_send.at[o], cf_recv.at[o], "freq", lax.rem(mf + o, nf)
         )
         for o in range(1, nf)
     ]
-    for copy in more:
-        copy.start()
-
-    predict(ITERS, resid_out)
+
+    def project():
+        for c in range(2):
+            for kk in range(kb):
+                both = gains[ITERS, c, own + kk] + dual[c, own + kk]
+                for j in range(NPOLY):
+                    row = (c * NPOLY + j) * kb + kk
+                    c_fr[mf, row : row + 1, :] = jnp.sum(basis[j] * both, axis=0, keepdims=True)
+        for n, (a, b) in enumerate(grams):
+            entry = jnp.sum(basis[a] * basis[b], axis=0, keepdims=True)
+            c_fr[mf, rows + n : rows + n + 1, :] = jnp.broadcast_to(entry, (1, stations))
+        for row in range(rows + len(grams), c_fr.shape[1]):
+            c_fr[mf, row : row + 1, :] = jnp.zeros((1, stations), jnp.float32)
+        for copy in more:
+            copy.start()
+
+    misfit = lax.fori_loop(0, ITERS - 1, iteration, predict(0, err, None))
+    iteration(ITERS - 1, misfit, resid_out, project)
     gains_out[...] = gains[ITERS]
 
     for copy in more:
@@ -401,7 +415,7 @@
         c_bl[me, row : row + 1, :] = jnp.zeros((1, stations), jnp.float32)
     spread = [
         remote(
-            c_bl.at[me], c_bl.at[me], cb_send.at[o], cb_recv.at[o], "bl", lax.rem(me + o, nb)
+            c_bl.at[me], c_bl.at[me], cb_send.at[o], cb_recv.at[o], "bl", bl_peer(o)
         )
         for o in range(1, nb)
     ]
@@ -453,7 +467,7 @@
             pltpu.VMEM((stations, 2 * base), bf16),
             pltpu.VMEM((2, dirn, slots, chans, base), f32),
             pltpu.VMEM((2, dirn, chans, 2 * base), f32),
-            pltpu.VMEM((2, 2 * dirn * chans, stations), bf16),
+            pltpu.VMEM((nb, 2, 2 * kb * chans, stations), bf16),
             pltpu.VMEM((2, slots, chans, base), f32),
             pltpu.VMEM((2, slots, chans, base), f32),
             pltpu.VMEM((chans, base), f32),

time: 129 us -> 126 us (0.977)
  Pallas kernels: 124 us -> 121 us
    pallas_call x1, Pallas kernels: 124 us -> 121 us  [body(): pl.pallas_call(functools.partial(kernel, sizes), name='admm_step', out_sh...]
where the time goes in v2:
time: 126 us
  Pallas kernels  121 us (96%)
  local copies, waits for them, and re-layouts  4.62 us (4%)
    pallas_call x1, Pallas kernels, body(): pl.pallas_call(functools.partial(kernel, sizes), name='admm_step', out_sh...  121 us
    unnamed x10, local copies, waits for them, and re-layouts  4.62 us

profile of v2, /device:TPU:0, one launch (start us, length us, event | category | flops | bytes accessed | tf_op | source)
XLA Modules:
  0.0 126.1 jit_solution(5959169375844212669)
XLA Ops:
  0.6 120.8 %admm_step.1 = (f32[2,8,16,512]{3,2,1,0:T(8,128)}, f32[2,3,8,512]{3,2,1,0:T(8,128)}, f32[2,8,16,512]{3,2,1,0:T(8,128)}, f32[2,2,16,2048]{3,2,1,0:T(8,128)}) custom-call(f32[2,2,16,2048]{3,2,1,0:T(8,128)} %vis.1, s32[2,16,2048]{2,1,0:T(8,128)} %flag.1, s32[2,2048]{1,0:T(2,128)} %pair.1, f32[2,2,2048]{2,1,0:T(2,128)} %coords.1, f32[2,8]{1,0:T(2,128)} %dirs.1, ...), custom_call_target="tpu_custom_call" | custom-call | tf_op jit(solution)/shard_map/admm_step/pallas_call | solution.py:455
  121.4 0.0 copy-start.2
  121.4 0.0 copy-start.1
  121.4 1.9 %copy.19 = f32[2,8,16,512]{3,2,1,0:T(8,128)} copy(f32[2,8,16,512]{3,2,1,0:T(8,128)} %get-tuple-element.8) | data formatting | bytes 1048576
  123.4 0.0 copy-done.2
  123.4 0.6 copy.20
  124.0 0.0 copy-done.1
  124.0 0.0 copy-start
  124.0 0.8 copy.21
  124.8 0.4 copy-done
  125.3 0.8 copy.22
Async XLA Ops:
  121.4 2.0 %copy-start.2 = (f32[2,3,8,512]{3,2,1,0:T(8,128)S(1)}, f32[2,3,8,512]{3,2,1,0:T(8,128)}, u32[]{:S(2)}) copy-start(f32[2,3,8,512]{3,2,1,0:T(8,128)} %get-tuple-element.9) | copy-start | bytes 294916
  121.4 2.6 %copy-start.1 = (f32[2,8,16,512]{3,2,1,0:T(8,128)S(1)}, f32[2,8,16,512]{3,2,1,0:T(8,128)}, u32[]{:S(2)}) copy-start(f32[2,8,16,512]{3,2,1,0:T(8,128)} %get-tuple-element.10) | copy-start | bytes 1572868
  124.0 1.2 copy-start

commit v3 on v2

--- a/solution.py
+++ b/solution.py
@@ -163,7 +163,7 @@
 
     count = lax.fori_loop(0, chunks, setup, jnp.zeros((8, 128), jnp.float32))
     for it in range(ITERS):
-        s_bl[it, me, 1] = count
+        s_bl[it, me, 1:2] = jnp.sum(count, axis=0, keepdims=True)
     gains[0] = gains_in[...]
 
     pl.semaphore_wait(barrier, nb + nf - 2)
@@ -219,7 +219,7 @@
         return remote(block, block, ag_send.at[it - 1, o], ag_recv.at[it - 1, o], "bl", bl_peer(o))
 
     def iteration(it, misfit, target=err, rhs_hook=None):
-        s_bl[it, me, 0] = misfit
+        s_bl[it, me, 0:1] = jnp.sum(misfit, axis=0, keepdims=True)
         copies = [
             remote(
                 s_bl.at[it, me], s_bl.at[it, me], sb_send.at[it, o], sb_recv.at[it, o],
@@ -249,9 +249,8 @@
         total = s_fr[it, 0]
         for o in range(1, nf):
             total = total + s_fr[it, o]
-        lanes = jnp.sum(total, axis=2, keepdims=True)
-        sums = jnp.sum(lanes, axis=1, keepdims=True)
-        sigma_sq = sums[0] / (sums[1] + 1.0) + small_term
+        sums = jnp.sum(total, axis=1, keepdims=True)
+        sigma_sq = sums[0:1] / (sums[1:2] + 1.0) + small_term
         inverse = 1.0 / sigma_sq
 
         def weigh(i, carry):
@@ -476,8 +475,8 @@
             pltpu.VMEM((ITERS, nb, 3, kb, chans, stations), f32),
             pltpu.VMEM((ITERS, nb, 3, kb, chans, stations), f32),
             pltpu.VMEM((ITERS + 1,) + gains.shape, f32),
-            pltpu.VMEM((ITERS, nb, 2, 8, 128), f32),
-            pltpu.VMEM((ITERS, nf, 2, 8, 128), f32),
+            pltpu.VMEM((ITERS, nb, 2, 128), f32),
+            pltpu.VMEM((ITERS, nf, 2, 128), f32),
             pltpu.VMEM((nf, pad(rows + 6), stations), f32),
             pltpu.VMEM((nb, pad(rows), stations), f32),
             dma((ITERS, nb)),

time: 126 us -> 126 us (level)
  no operation moved by 1% of the time
where the time goes in v3:
time: 126 us
  Pallas kernels  120 us (95%)
  local copies, waits for them, and re-layouts  4.62 us (4%)
    pallas_call x1, Pallas kernels, body(): pl.pallas_call(functools.partial(kernel, sizes), name='admm_step', out_sh...  120 us
    unnamed x10, local copies, waits for them, and re-layouts  4.62 us

profile of v3, /device:TPU:0, one launch (start us, length us, event | category | flops | bytes accessed | tf_op | source)
XLA Modules:
  0.0 125.7 jit_solution(5033563970635641761)
XLA Ops:
  0.6 120.5 %admm_step.1 = (f32[2,8,16,512]{3,2,1,0:T(8,128)}, f32[2,3,8,512]{3,2,1,0:T(8,128)}, f32[2,8,16,512]{3,2,1,0:T(8,128)}, f32[2,2,16,2048]{3,2,1,0:T(8,128)}) custom-call(f32[2,2,16,2048]{3,2,1,0:T(8,128)} %vis.1, s32[2,16,2048]{2,1,0:T(8,128)} %flag.1, s32[2,2048]{1,0:T(2,128)} %pair.1, f32[2,2,2048]{2,1,0:T(2,128)} %coords.1, f32[2,8]{1,0:T(2,128)} %dirs.1, ...), custom_call_target="tpu_custom_call" | custom-call | tf_op jit(solution)/shard_map/admm_step/pallas_call | solution.py:454
  121.1 0.0 copy-start.2
  121.1 0.0 copy-start.1
  121.1 1.9 %copy.19 = f32[2,8,16,512]{3,2,1,0:T(8,128)} copy(f32[2,8,16,512]{3,2,1,0:T(8,128)} %get-tuple-element.8) | data formatting | bytes 1048576
  123.1 0.0 copy-done.2
  123.1 0.6 copy.20
  123.7 0.0 copy-done.1
  123.7 0.0 copy-start
  123.7 0.8 copy.21
  124.5 0.4 copy-done
  124.9 0.8 copy.22
Async XLA Ops:
  121.1 2.0 %copy-start.2 = (f32[2,3,8,512]{3,2,1,0:T(8,128)S(1)}, f32[2,3,8,512]{3,2,1,0:T(8,128)}, u32[]{:S(2)}) copy-start(f32[2,3,8,512]{3,2,1,0:T(8,128)} %get-tuple-element.9) | copy-start | bytes 294916
  121.1 2.6 %copy-start.1 = (f32[2,8,16,512]{3,2,1,0:T(8,128)S(1)}, f32[2,8,16,512]{3,2,1,0:T(8,128)}, u32[]{:S(2)}) copy-start(f32[2,8,16,512]{3,2,1,0:T(8,128)} %get-tuple-element.10) | copy-start | bytes 1572868
  123.7 1.2 copy-start
